TPU v7x, 256 devices: a whole 4x4x8 slice. The times are simulated.
256 devices in a mesh: nodes: 128 (over y, z, x), rep: 2 (over core).
Axes of the slice: x: 4, y: 4, z: 8, core: 2. Of those that a mesh axis runs over, the one named last changes fastest.
Arguments:
- node_latent: bfloat16 [40960, 512], P(('nodes', 'rep')), may hold values from -6 to 6
- edge_saved: bfloat16 [327680, 512], P(('nodes', 'rep')), may hold values from -6 to 6
- node_cot: bfloat16 [40960, 512], P(('nodes', 'rep')), may hold values from -6 to 6
- edge_cot: bfloat16 [327680, 512], P(('nodes', 'rep')), may hold values from -6 to 6
- senders: int32 [327680], P(('nodes', 'rep')), may hold values from 0 to 1343, as said below
- receivers: int32 [327680], P(('nodes', 'rep')), may hold values from 0 to 319
- ghost_rows: int32 [128, 128, 8], P('nodes'), may hold values from 0 to 319, as said below
- w_edge_in: bfloat16 [1536, 512], replicated, may hold values from -0.15625 to 0.15625
- w_edge_out: bfloat16 [512, 512], replicated, may hold values from -0.25 to 0.25
- edge_gain: float32 [512], replicated, may hold values from 0.5 to 2
- edge_offset: float32 [512], replicated, may hold values from -3 to 3
- w_node_in: bfloat16 [1024, 512], replicated, may hold values from -0.1875 to 0.1875
- w_node_out: bfloat16 [512, 512], replicated, may hold values from -0.25 to 0.25
- node_gain: float32 [512], replicated, may hold values from 0.5 to 2
Outputs:
- grad_nodes: bfloat16 [40960, 512], P(('nodes', 'rep'))
- grad_edges: bfloat16 [327680, 512], P(('nodes', 'rep'))
- grad_edge_in: bfloat16 [1536, 512], replicated
- grad_edge_out: bfloat16 [512, 512], replicated
- grad_node_in: bfloat16 [1024, 512], replicated
- grad_node_out: bfloat16 [512, 512], replicated
Inputs may be any that keep to these rules, and one draw needn't show every extreme that they name: `senders`: A sender below 320 is a node of the edge's own partition; otherwise it is 320 + q * 8 + s, the ghost slot s of the list of a partition q other than the edge's own. Each list ghost_rows[q, p] holds 8 distinct rows.
All inputs are finite; a program needn't handle non-finite values.
Results may differ from a plain program's by a relative error of at most 0.008.
Values may be sent and summed in bfloat16 or wider, within the bound.
No kernel may reach another device: no remote copies, remote signals or barrier semaphores. Data moves between devices by JAX's collectives and lax.ppermute only.
A program may use at most 128 MiB of HBM per device.

v0:
```python
import math
import jax
import jax.numpy as jnp
from jax import lax
from jax.sharding import PartitionSpec as P

EPS = 1e-05


def swapped(array, axis, bit):
    return lax.ppermute(array, axis, [(i, i ^ 1 << bit) for i in range(lax.axis_size(axis))])


def sent_to_all(array, axis):
    devices = lax.axis_size(axis)
    return lax.all_to_all(
        jnp.broadcast_to(array[None], (devices, *array.shape)), axis, 0, 0, tiled=True
    )


def in_order(blocks, dim):
    blocks = jnp.moveaxis(blocks, 0, dim)
    dims = blocks.shape
    return blocks.reshape(*dims[:dim], dims[dim] * dims[dim + 1], *dims[dim + 2 :])


def gather_directly(array, axis, dim):
    blocks = sent_to_all(array, axis)
    return in_order(blocks, dim)


def split_up(array, dim, devices):
    before, after = (array.shape[:dim], array.shape[dim + 1 :])
    return jnp.moveaxis(array.reshape(*before, devices, -1, *after), dim, 0)


def summed_on_arrival(array, axis, dim):
    devices = lax.axis_size(axis)
    blocks = lax.all_to_all(split_up(array, dim, devices), axis, 0, 0, tiled=True)
    return jnp.sum(blocks, axis=0)


def summed_on_arrival_2(array, axis, dim):
    devices = lax.axis_size(axis)
    blocks = lax.all_to_all(split_up(array, dim, devices), axis, 0, 0, tiled=True)
    return jnp.sum(blocks.astype(jnp.float32), axis=0)


def mat_mul(left, right):
    return jnp.dot(left, right, preferred_element_type=jnp.float32)


def mat_tn(left, right):
    return lax.dot_general(
        left, right, (((0,), (0,)), ((), ())), preferred_element_type=jnp.float32
    )


def mat_nt(left, right):
    return lax.dot_general(
        left, right, (((1,), (1,)), ((), ())), preferred_element_type=jnp.float32
    )


def silu_slope(value):
    sigmoid_v = jax.nn.sigmoid(value)
    return sigmoid_v * (1.0 + value * (1.0 - sigmoid_v))


def norm_forward(value):
    centred = value - jnp.mean(value, axis=-1, keepdims=True)
    inverse = lax.rsqrt(jnp.mean(centred * centred, axis=-1, keepdims=True) + EPS)
    return (centred * inverse, inverse)


def norm_backward(grad_hat, normed, inverse):
    return inverse * (
        grad_hat
        - jnp.mean(grad_hat, axis=-1, keepdims=True)
        - normed * jnp.mean(grad_hat * normed, axis=-1, keepdims=True)
    )


def edge_forward(edge_block, send_rows, recv_rows, w_edge_in, w_edge_out, edge_gain, edge_offset):
    latent_width = edge_block.shape[1]
    pre_act = (
        mat_mul(edge_block, w_edge_in[:latent_width])
        + mat_mul(send_rows, w_edge_in[latent_width : 2 * latent_width])
        + mat_mul(recv_rows, w_edge_in[2 * latent_width :])
    )
    edge_hidden = jax.nn.silu(pre_act).astype(jnp.bfloat16)
    edge_normed, edge_inverse = norm_forward(mat_mul(edge_hidden, w_edge_out))
    message = edge_normed * edge_gain + edge_offset
    return (pre_act, edge_hidden, edge_normed, edge_inverse, message)


def edge_backward(
    edge_block,
    send_rows,
    recv_rows,
    edge_cot,
    message_grad,
    saved,
    w_edge_in,
    w_edge_out,
    edge_gain,
):
    pre_act, edge_hidden, edge_normed, edge_inverse = saved
    latent_width = edge_block.shape[1]
    grad_out = norm_backward(message_grad * edge_gain, edge_normed, edge_inverse).astype(
        jnp.bfloat16
    )
    grad_act = (mat_nt(grad_out, w_edge_out) * silu_slope(pre_act)).astype(jnp.bfloat16)
    in_grad = jnp.concatenate(
        [mat_tn(edge_block, grad_act), mat_tn(send_rows, grad_act), mat_tn(recv_rows, grad_act)], 0
    )
    out_grad = mat_tn(edge_hidden, grad_out)
    edge_grad = (edge_cot.astype(jnp.float32) + mat_nt(grad_act, w_edge_in[:latent_width])).astype(
        jnp.bfloat16
    )
    send_grad = mat_nt(grad_act, w_edge_in[latent_width : 2 * latent_width])
    recv_grad = mat_nt(grad_act, w_edge_in[2 * latent_width :])
    return (edge_grad, send_grad, recv_grad, in_grad, out_grad)


def node_pass(node_rows, totals_b, node_cot, w_node_in, w_node_out, node_gain):
    latent_width = node_rows.shape[1]
    node_pre = mat_mul(node_rows, w_node_in[:latent_width]) + mat_mul(
        totals_b, w_node_in[latent_width:]
    )
    node_hidden = jax.nn.silu(node_pre).astype(jnp.bfloat16)
    node_normed, node_inverse = norm_forward(mat_mul(node_hidden, w_node_out))
    grad_out = norm_backward(
        node_cot.astype(jnp.float32) * node_gain, node_normed, node_inverse
    ).astype(jnp.bfloat16)
    grad_act = (mat_nt(grad_out, w_node_out) * silu_slope(node_pre)).astype(jnp.bfloat16)
    in_grad = jnp.concatenate([mat_tn(node_rows, grad_act), mat_tn(totals_b, grad_act)], 0)
    direct_grad = mat_nt(grad_act, w_node_in[:latent_width])
    totals_grad = mat_nt(grad_act, w_node_in[latent_width:]).astype(jnp.bfloat16)
    return (direct_grad, totals_grad, in_grad, mat_tn(node_hidden, grad_out))


def shards(
    node_latent,
    edge_saved,
    node_cot,
    edge_cot,
    senders,
    receivers,
    ghost_rows,
    w_edge_in,
    w_edge_out,
    edge_gain,
    edge_offset,
    w_node_in,
    w_node_out,
    node_gain,
):
    latent_width = node_latent.shape[1]
    edge_latent = swapped(edge_saved, "rep", 0)
    partition = gather_directly(node_latent, "rep", 0)
    part_rows = partition.shape[0]
    ghost_lists = ghost_rows[0]
    part_count = ghost_lists.shape[0]
    slot_count = ghost_lists.shape[1]
    half_slots = slot_count // lax.axis_size("rep")
    own_lists = lax.dynamic_slice_in_dim(
        ghost_lists, lax.axis_index("rep") * half_slots, half_slots, 1
    )
    outgoing = partition[own_lists.reshape(-1)].reshape(part_count, half_slots, latent_width)
    arrived = lax.all_to_all(outgoing, "nodes", split_axis=0, concat_axis=0, tiled=True)
    ghosts = gather_directly(arrived, "rep", 1)
    node_table = jnp.concatenate(
        [partition, ghosts.reshape(part_count * slot_count, latent_width)], 0
    )
    send_rows = node_table[senders]
    recv_rows = partition[receivers]
    pre_act, edge_hidden, edge_normed, edge_inverse, message = edge_forward(
        edge_latent, send_rows, recv_rows, w_edge_in, w_edge_out, edge_gain, edge_offset
    )
    partial_totals = jax.ops.segment_sum(message, receivers, num_segments=part_rows)
    totals = summed_on_arrival(partial_totals, "rep", 0)
    direct_grad, totals_grad, node_in_grad, node_out_grad = node_pass(
        node_latent, totals.astype(jnp.bfloat16), node_cot, w_node_in, w_node_out, node_gain
    )
    partition_totals_grad = gather_directly(totals_grad, "rep", 0)
    message_grad = edge_cot.astype(jnp.float32) + partition_totals_grad[receivers].astype(
        jnp.float32
    )
    edge_grad, send_grad, recv_grad, edge_in_grad, edge_out_grad = edge_backward(
        edge_latent,
        send_rows,
        recv_rows,
        edge_cot,
        message_grad,
        (pre_act, edge_hidden, edge_normed, edge_inverse),
        w_edge_in,
        w_edge_out,
        edge_gain,
    )
    table_grad = jax.ops.segment_sum(send_grad, senders, num_segments=node_table.shape[0])
    row_grad = table_grad[:part_rows] + jax.ops.segment_sum(
        recv_grad, receivers, num_segments=part_rows
    )
    ghost_grad = table_grad[part_rows:].reshape(part_count, slot_count, latent_width)
    paired = summed_on_arrival_2(ghost_grad.astype(jnp.bfloat16), "rep", 1)
    returned = lax.all_to_all(
        paired.astype(jnp.bfloat16), "nodes", split_axis=0, concat_axis=0, tiled=True
    ).astype(paired.dtype)
    row_grad = row_grad + jax.ops.segment_sum(
        returned.reshape(-1, latent_width), own_lists.reshape(-1), num_segments=part_rows
    )
    own_grad = summed_on_arrival(row_grad, "rep", 0)
    grad_nodes = (own_grad + direct_grad + node_cot.astype(jnp.float32)).astype(jnp.bfloat16)
    weight_grads = (edge_in_grad, edge_out_grad, node_in_grad, node_out_grad)
    device_count = lax.axis_size("nodes") * lax.axis_size("rep")
    edge_scale = 1.0 / math.sqrt(senders.shape[0] * device_count)
    node_scale = 1.0 / math.sqrt(node_latent.shape[0] * device_count)
    weight_total = lax.psum(
        (weight_grads[0], weight_grads[1], weight_grads[2], weight_grads[3]), ("nodes", "rep")
    )
    return (
        grad_nodes,
        edge_grad,
        (weight_total[0] * edge_scale).astype(jnp.bfloat16),
        (weight_total[1] * edge_scale).astype(jnp.bfloat16),
        (weight_total[2] * node_scale).astype(jnp.bfloat16),
        (weight_total[3] * node_scale).astype(jnp.bfloat16),
    )


def solution(mesh):
    return jax.shard_map(
        shards,
        mesh=mesh,
        in_specs=(
            P(("nodes", "rep"), None),
            P(("nodes", "rep"), None),
            P(("nodes", "rep"), None),
            P(("nodes", "rep"), None),
            P(("nodes", "rep")),
            P(("nodes", "rep")),
            P("nodes", None, None),
            P(),
            P(),
            P(),
            P(),
            P(),
            P(),
            P(),
        ),
        out_specs=(P(("nodes", "rep"), None), P(("nodes", "rep"), None), P(), P(), P(), P()),
        check_vma=False,
    )
```

profile of v0, /device:TPU:2, one launch (start us, length us, event | category | flops | bytes accessed | tf_op | source)
XLA Modules:
  0.0 423.5 jit_solution(2287839622179952610)
XLA Ops:
  8.9 3.5 all-to-all-start
  16.8 15.9 %all-to-all-start.1 = ((bf16[128,4,512]{2,1,0:T(4,128)(2,1)}), bf16[128,4,512]{2,1,0:T(4,128)(2,1)}, u32[]{:S(2)}, u32[]{:S(2)}) async-start(bf16[128,4,512]{2,1,0:T(4,128)(2,1)} %reshape.119), calls=%async_computation.1 | async-start | bytes 1048576 | tf_op jit(solution)/shard_map/all_to_all | solution.py:171
  32.9 4.1 gather_fusion.2
  37.1 2.9 copy.33
  41.6 3.4 fusion.17
  45.0 6.5 %all-to-all-done.1 = bf16[128,4,512]{2,1,0:T(4,128)(2,1)} async-done(((bf16[128,4,512]{2,1,0:T(4,128)(2,1)}), bf16[128,4,512]{2,1,0:T(4,128)(2,1)}, u32[]{:S(2)}, u32[]{:S(2)}) %all-to-all-start.1) | async-done | bytes 524320 | tf_op jit(solution)/shard_map/all_to_all | solution.py:171
  52.8 5.1 %all_to_all.40 = bf16[2,128,4,512]{3,2,1,0:T(4,128)(2,1)S(1)} all-to-all(bf16[2,128,4,512]{3,2,1,0:T(4,128)(2,1)S(1)} %broadcast_in_dim.19), channel_id=1, replica_groups=mesh['nodes'=128,'rep'=2] {'rep'}, dimensions={0} | all-to-all | bytes 2097152 | tf_op jit(solution)/shard_map/all_to_all | solution.py:16
  58.7 4.2 %gather_fusion.1 = bf16[1280,512]{1,0:T(8,128)(2,1)S(1)} fusion(bf16[1344,512]{1,0:T(8,128)(2,1)S(1)} %pad_maximum_fusion.2, s32[2048]{0:T(1024)} %pad_clamp_fusion.1), kind=kCustom, calls=%fused_computation.1 | custom fusion | bytes 2626560 | tf_op jit(solution)/shard_map/gather | solution.py:176
  65.4 4.2 %multiply_convert_fusion.2 = (bf16[1280,512]{1,0:T(8,128)(2,1)S(1)}, f32[1280,512]{1,0:T(8,128)}) fusion(f32[1280,512]{1,0:T(8,128)S(1)} %copy-done.10, f32[1280,512]{1,0:T(8,128)S(1)} %fusion.21, bf16[1280,512]{1,0:T(8,128)(2,1)} %collective-permute-done, bf16[1536,512]{1,0:T(8,128)(2,1)} %param.21), kind=kOutput, calls=%fused_computation.22 | convolution fusion | flops 675676160 | bytes 11010048 | tf_op jit(solution)/shard_map/dot_general | solution.py:50
  72.8 3.2 copy.34
  76.0 11.1 %scatter_custom_fusion = f32[320,512]{1,0:T(8,128)} fusion(s32[1280]{0:T(1024)S(1)} %copy-done.35, f32[1280,512]{1,0:T(8,128)} %copy.34, f32[]{:T(128)} %constant.13.clone.1), kind=kCustom, calls=%fused_computation.72 | custom fusion | flops 655360 | bytes 655872 | tf_op jit(solution)/shard_map/scatter-add | solution.py:181
  87.1 6.4 %all_to_all.41 = f32[2,160,512]{2,1,0:T(8,128)} all-to-all(f32[2,160,512]{2,1,0:T(8,128)} %bitcast.47), channel_id=1, replica_groups=mesh['nodes'=128,'rep'=2] {'rep'}, dimensions={0} | all-to-all | bytes 1310720 | tf_op jit(solution)/shard_map/all_to_all | solution.py:39
  99.3 4.2 all_to_all.42
  103.5 4.7 %gather_fusion.3 = bf16[1280,512]{1,0:T(8,128)(2,1)} fusion(bf16[320,512]{1,0:T(8,128)(2,1)S(1)} %bitcast.44, s32[2048]{0:T(1024)S(1)} %pad_clamp_fusion), kind=kCustom, calls=%fused_computation.3 | custom fusion | bytes 2626560 | tf_op jit(solution)/shard_map/gather | solution.py:187
  129.9 3.5 fusion.19
  133.4 11.1 %scatter_custom_fusion.1 = f32[1344,512]{1,0:T(8,128)S(1)} fusion(s32[1280]{0:T(1024)} %param.18, f32[1280,512]{1,0:T(8,128)} %fusion.19, f32[]{:T(128)} %constant.13.clone.1), kind=kCustom, calls=%fused_computation.30 | custom fusion | flops 655360 | bytes 2753024 | tf_op jit(solution)/shard_map/scatter-add | solution.py:201
  149.6 5.6 %all_to_all.43 = bf16[2,128,4,512]{3,2,1,0:T(4,128)(2,1)} all-to-all(bf16[2,128,4,512]{3,2,1,0:T(4,128)(2,1)S(1)} %bitcast.46), channel_id=1, replica_groups=mesh['nodes'=128,'rep'=2] {'rep'}, dimensions={0} | all-to-all | bytes 2097152 | tf_op jit(solution)/shard_map/all_to_all | solution.py:45
  158.1 8.1 %all-to-all-start.6 = ((bf16[128,4,512]{2,1,0:T(4,128)(2,1)}), bf16[128,4,512]{2,1,0:T(4,128)(2,1)}, u32[]{:S(2)}, u32[]{:S(2)}) async-start(bf16[128,4,512]{2,1,0:T(4,128)(2,1)} %reduce_sum.111), calls=%async_computation.6 | async-start | bytes 1048576 | tf_op jit(solution)/shard_map/all_to_all | solution.py:207
  173.0 9.9 %scatter_fusion = f32[320,512]{1,0:T(8,128)S(1)} fusion(f32[320,512]{1,0:T(8,128)S(1)} %slice-done, s32[1280]{0:T(1024)S(1)} %copy-done.35, f32[1280,512]{1,0:T(8,128)S(1)} %fusion.15), kind=kCustom, calls=%fused_computation.6 | custom fusion | flops 655360 | bytes 7869440 | tf_op jit(solution)/shard_map/scatter-add | solution.py:202
  182.9 4.6 %all-to-all-done.6 = bf16[128,4,512]{2,1,0:T(4,128)(2,1)} async-done(((bf16[128,4,512]{2,1,0:T(4,128)(2,1)}), bf16[128,4,512]{2,1,0:T(4,128)(2,1)}, u32[]{:S(2)}, u32[]{:S(2)}) %all-to-all-start.6) | async-done | bytes 524320 | tf_op jit(solution)/shard_map/all_to_all | solution.py:207
  189.5 4.8 %scatter_custom_fusion.3 = f32[320,512]{1,0:T(8,128)S(1)} fusion(s32[512]{0:T(512)S(1)} %reshape.185, f32[512,512]{1,0:T(8,128)} %reshape.187, f32[]{:T(128)} %constant.13.clone.1), kind=kCustom, calls=%fused_computation.70 | custom fusion | flops 262144 | bytes 655872 | tf_op jit(solution)/shard_map/scatter-add | solution.py:210
  194.4 4.3 %all_to_all.44 = f32[2,160,512]{2,1,0:T(8,128)S(1)} all-to-all(f32[2,160,512]{2,1,0:T(8,128)S(1)} %bitcast.48), channel_id=1, replica_groups=mesh['nodes'=128,'rep'=2] {'rep'}, dimensions={0} | all-to-all | bytes 1310720 | tf_op jit(solution)/shard_map/all_to_all | solution.py:39
  199.7 209.9 %all-reduce.3.cloned.1.call-done = (f32[1536,512]{1,0:T(8,128)}, f32[512,512]{1,0:T(8,128)}, f32[1024,512]{1,0:T(8,128)}, f32[512,512]{1,0:T(8,128)}) async-done(((f32[1536,512]{1,0:T(8,128)}, f32[512,512]{1,0:T(8,128)}, f32[1024,512]{1,0:T(8,128)}, f32[512,512]{1,0:T(8,128)}), (f32[1536,512]{1,0:T(8,128)}, f32[512,512]{1,0:T(8,128)}, f32[1024,512]{1,0:T(8,128)}, ...) | async-done | bytes 7340048 | tf_op jit(solution)/shard_map/psum | solution.py:219
  409.7 3.6 multiply_convert_fusion
  (163 shorter events, 63.9 us)
Async XLA Ops:
  7.2 62.4 %copy-start = (bf16[512,512]{1,0:T(8,128)(2,1)S(1)}, bf16[512,512]{1,0:T(8,128)(2,1)}, u32[]{:S(2)}) copy-start(bf16[512,512]{1,0:T(8,128)(2,1)} %param.22) | copy-start | bytes 1572868
  8.9 5.0 %all-to-all-start = ((bf16[2,160,512]{2,1,0:T(8,128)(2,1)}), bf16[2,160,512]{2,1,0:T(8,128)(2,1)S(1)}, u32[]{:S(2)}, u32[]{:S(2)}) async-start(bf16[2,160,512]{2,1,0:T(8,128)(2,1)} %broadcast_in_dim.18), calls=%async_computation | async-start | bytes 655360 | tf_op jit(solution)/shard_map/all_to_all | solution.py:16
  14.0 18.9 %copy-start.35 = (s32[1280]{0:T(1024)S(1)}, s32[1280]{0:T(1024)}, u32[]{:S(2)}) copy-start(s32[1280]{0:T(1024)} %param.19) | copy-start | bytes 15364
  16.8 34.7 %all-to-all-start.1 = ((bf16[128,4,512]{2,1,0:T(4,128)(2,1)}), bf16[128,4,512]{2,1,0:T(4,128)(2,1)}, u32[]{:S(2)}, u32[]{:S(2)}) async-start(bf16[128,4,512]{2,1,0:T(4,128)(2,1)} %reshape.119), calls=%async_computation.1 | async-start | bytes 1048576 | tf_op jit(solution)/shard_map/all_to_all | solution.py:171
  32.7 376.9 %all-reduce.3.cloned.1.call-start = ((), (), s32[]{:S(2)}) async-start(), calls=%async_computation.8 | async-start | bytes 14680064 | tf_op jit(solution)/shard_map/psum | solution.py:219
  32.8 32.5 %collective-permute-start = (bf16[1280,512]{1,0:T(8,128)(2,1)}, bf16[1280,512]{1,0:T(8,128)(2,1)}, u32[]{:S(2)}, u32[]{:S(2)}) collective-permute-start(bf16[1280,512]{1,0:T(8,128)(2,1)} %param.15), channel_id=1, source_target_pairs={{0,1},{1,0},{2,3},{3,2},{4,5},{5,4},{6,7},{7,6},{8,9},{9,8},{10,11... | collective-permute-start | bytes 3932168 | tf_op jit(solution)/shard_map/ppermute | solution.py:11
  37.0 7.9 %copy-start.5 = (bf16[1280,512]{1,0:T(8,128)(2,1)}, bf16[1280,512]{1,0:T(8,128)(2,1)S(1)}, u32[]{:S(2)}) copy-start(bf16[1280,512]{1,0:T(8,128)(2,1)S(1)} %gather_fusion.2) | copy-start | bytes 3932164
  62.9 6.7 %copy-start.7 = (bf16[1280,512]{1,0:T(8,128)(2,1)}, bf16[1280,512]{1,0:T(8,128)(2,1)S(1)}, u32[]{:S(2)}) copy-start(bf16[1280,512]{1,0:T(8,128)(2,1)S(1)} %gather_fusion.1) | copy-start | bytes 3932164
  87.1 10.8 %copy-start.27 = (bf16[160,512]{1,0:T(8,128)(2,1)S(1)}, bf16[160,512]{1,0:T(8,128)(2,1)}, u32[]{:S(2)}) copy-start(bf16[160,512]{1,0:T(8,128)(2,1)} %param.16) | copy-start | bytes 491524
  87.1 10.9 %copy-start.39 = (f32[512]{0:T(512)S(1)}, f32[512]{0:T(512)}, u32[]{:S(2)}) copy-start(f32[512]{0:T(512)} %param.27) | copy-start | bytes 6148
  94.6 4.0 copy-start.17
  94.6 3.6 copy-start.28
  94.7 3.6 copy-start.44
  97.7 5.8 %copy-start.21 = (f32[160,512]{1,0:T(8,128)}, f32[160,512]{1,0:T(8,128)S(1)}, u32[]{:S(2)}) copy-start(f32[160,512]{1,0:T(8,128)S(1)} %get-tuple-element.37) | copy-start | bytes 983044
  98.2 10.0 %copy-start.40 = (f32[160]{0:T(256)}, f32[160]{0:T(256)S(1)}, u32[]{:S(2)}) copy-start(f32[160]{0:T(256)S(1)} %get-tuple-element.38) | copy-start | bytes 1924
  98.2 10.0 %copy-start.42 = (f32[160]{0:T(256)}, f32[160]{0:T(256)S(1)}, u32[]{:S(2)}) copy-start(f32[160]{0:T(256)S(1)} %get-tuple-element.39) | copy-start | bytes 1924
  116.6 13.3 %copy-start.9 = (bf16[1280,512]{1,0:T(8,128)(2,1)}, bf16[1280,512]{1,0:T(8,128)(2,1)S(1)}, u32[]{:S(2)}) copy-start(bf16[1280,512]{1,0:T(8,128)(2,1)S(1)} %fusion.2) | copy-start | bytes 3932164
  144.5 21.8 %copy-start.2 = (f32[1344,512]{1,0:T(8,128)}, f32[1344,512]{1,0:T(8,128)S(1)}, u32[]{:S(2)}) copy-start(f32[1344,512]{1,0:T(8,128)S(1)} %scatter_custom_fusion.1) | copy-start | bytes 8257540
  149.6 16.6 %copy-start.32 = (s32[1,128,4]{2,1,0:T(8,128)S(1)}, s32[1,128,4]{2,1,0:T(8,128)}, u32[]{:S(2)}) copy-start(s32[1,128,4]{2,1,0:T(8,128)} %copy-done.31) | copy-start | bytes 6148
  158.1 29.4 %all-to-all-start.6 = ((bf16[128,4,512]{2,1,0:T(4,128)(2,1)}), bf16[128,4,512]{2,1,0:T(4,128)(2,1)}, u32[]{:S(2)}, u32[]{:S(2)}) async-start(bf16[128,4,512]{2,1,0:T(4,128)(2,1)} %reduce_sum.111), calls=%async_computation.6 | async-start | bytes 1048576 | tf_op jit(solution)/shard_map/all_to_all | solution.py:207
  189.5 9.2 %copy-start.13 = (bf16[1024,512]{1,0:T(8,128)(2,1)S(1)}, bf16[1024,512]{1,0:T(8,128)(2,1)}, u32[]{:S(2)}) copy-start(bf16[1024,512]{1,0:T(8,128)(2,1)} %param.25) | copy-start | bytes 3145732
  189.5 9.2 %copy-start.30 = (bf16[160,512]{1,0:T(8,128)(2,1)S(1)}, bf16[160,512]{1,0:T(8,128)(2,1)}, u32[]{:S(2)}) copy-start(bf16[160,512]{1,0:T(8,128)(2,1)} %param.16) | copy-start | bytes 491524
  409.7 3.6 copy-start.26
  409.7 4.6 %copy-start.14 = (f32[1024,512]{1,0:T(8,128)S(1)}, f32[1024,512]{1,0:T(8,128)}, u32[]{:S(2)}) copy-start(f32[1024,512]{1,0:T(8,128)} %get-tuple-element.30) | copy-start | bytes 6291460
  (28 other events, 53.5 us)
Sparse Core Ops, SparseCore 0:
  130.0 279.6 all-reduce.2
where the time goes:
time: 430 us; the launch traced here: 424 us
  waiting for transfers between devices  222 us (52%)
  other arithmetic  58.3 us (14%)
  local copies, waits for them, and re-layouts  40.9 us (10%)
  matrix products  34.6 us (8%)
  starting transfers between devices  27.6 us (6%)
  blocking collectives  25.5 us (6%)
  between operations  15 us (3%)
    psum x1, waiting for transfers between devices, shards(): lax.psum((weight_grads[0], weight_grads[1], weight_grads[2], weight_grads...  210 us
    all_to_all x1, starting transfers between devices, shards(): lax.all_to_all(outgoing, 'nodes', split_axis=0, concat_axis=0, tiled=True)  15.9 us
    dot_general x7, matrix products, mat_mul(): return jnp.dot(left, right, preferred_element_type=jnp.float32)  14.9 us
    dot_general x7, matrix products, mat_nt(): lax.dot_general(left, right, (((1,), (1,)), ((), ())), preferred_element_...  11.8 us
    scatter-add x1, other arithmetic, shards(): jax.ops.segment_sum(send_grad, senders, num_segments=node_table.shape[0])  11.1 us
    scatter-add x1, other arithmetic, shards(): jax.ops.segment_sum(message, receivers, num_segments=part_rows)  11.1 us
    all_to_all x2, blocking collectives, summed_on_arrival(): lax.all_to_all(split_up(array, dim, devices), axis, 0, 0, tiled=True)  10.6 us
    scatter-add x1, other arithmetic, shards(): jax.ops.segment_sum(recv_grad, receivers, num_segments=part_rows)  9.89 us
  transfers between devices with their start and end apart: 5, of which 4 were waited for; matrix products, arithmetic and copies ran while one was open for 16% of the time, Pallas kernels for 0%

commit v1 on v0

--- a/solution.py
+++ b/solution.py
@@ -216,9 +216,9 @@
     device_count = lax.axis_size("nodes") * lax.axis_size("rep")
     edge_scale = 1.0 / math.sqrt(senders.shape[0] * device_count)
     node_scale = 1.0 / math.sqrt(node_latent.shape[0] * device_count)
-    weight_total = lax.psum(
-        (weight_grads[0], weight_grads[1], weight_grads[2], weight_grads[3]), ("nodes", "rep")
-    )
+    weight_total = (weight_grads[0], weight_grads[1], weight_grads[2], weight_grads[3])
+    for over in ("nodes", "rep"):
+        weight_total = lax.psum(weight_total, over)
     return (
         grad_nodes,
         edge_grad,

time: 430 us -> 470 us (1.093)
  waiting for transfers between devices: 222 us -> 256 us
    psum x1 -> x2, waiting for transfers between devices: 210 us -> 248 us  [shards(): weight_total = lax.psum(weight_total, over)]
  transfers between devices with their start and end apart: 5 -> 6, of which waited for: 4 -> 4; matrix products, arithmetic and copies ran while one was open for 16% -> 15% of each run, Pallas kernels for 0% -> 0%
where the time goes in v1:
time: 470 us; the launch traced here: 462 us
  waiting for transfers between devices  256 us (54%)
  other arithmetic  58.1 us (12%)
  local copies, waits for them, and re-layouts  41.6 us (9%)
  matrix products  35 us (7%)
  starting transfers between devices  31 us (7%)
  blocking collectives  25.5 us (5%)
  between operations  15 us (3%)
    psum x2, waiting for transfers between devices, shards(): weight_total = lax.psum(weight_total, over)  248 us
    all_to_all x1, starting transfers between devices, shards(): lax.all_to_all(outgoing, 'nodes', split_axis=0, concat_axis=0, tiled=True)  15.9 us
    dot_general x7, matrix products, mat_mul(): return jnp.dot(left, right, preferred_element_type=jnp.float32)  14.9 us
    dot_general x7, matrix products, mat_nt(): lax.dot_general(left, right, (((1,), (1,)), ((), ())), preferred_element_...  12.2 us
    all_to_all x1, starting transfers between devices, shards(): lax.all_to_all(paired.astype(jnp.bfloat16), 'nodes', split_axis=0, concat...  11.3 us
    scatter-add x1, other arithmetic, shards(): jax.ops.segment_sum(message, receivers, num_segments=part_rows)  11.1 us
    scatter-add x1, other arithmetic, shards(): jax.ops.segment_sum(send_grad, senders, num_segments=node_table.shape[0])  10.9 us
    all_to_all x2, blocking collectives, summed_on_arrival(): lax.all_to_all(split_up(array, dim, devices), axis, 0, 0, tiled=True)  10.6 us
  transfers between devices with their start and end apart: 6, of which 4 were waited for; matrix products, arithmetic and copies ran while one was open for 15% of the time, Pallas kernels for 0%

profile of v1, /device:TPU:2, one launch (start us, length us, event | category | flops | bytes accessed | tf_op | source)
XLA Modules:
  0.0 462.4 jit_solution(16204627394645984807)
XLA Ops:
  8.9 3.5 all-to-all-start
  16.8 15.9 %all-to-all-start.1 = ((bf16[128,4,512]{2,1,0:T(4,128)(2,1)}), bf16[128,4,512]{2,1,0:T(4,128)(2,1)}, u32[]{:S(2)}, u32[]{:S(2)}) async-start(bf16[128,4,512]{2,1,0:T(4,128)(2,1)} %reshape.119), calls=%async_computation.1 | async-start | bytes 1048576 | tf_op jit(solution)/shard_map/all_to_all | solution.py:171
  32.9 4.1 gather_fusion.2
  37.1 2.9 copy.33
  41.6 3.4 fusion.17
  45.0 6.5 %all-to-all-done.1 = bf16[128,4,512]{2,1,0:T(4,128)(2,1)} async-done(((bf16[128,4,512]{2,1,0:T(4,128)(2,1)}), bf16[128,4,512]{2,1,0:T(4,128)(2,1)}, u32[]{:S(2)}, u32[]{:S(2)}) %all-to-all-start.1) | async-done | bytes 524320 | tf_op jit(solution)/shard_map/all_to_all | solution.py:171
  52.8 4.9 %all_to_all.40 = bf16[2,128,4,512]{3,2,1,0:T(4,128)(2,1)S(1)} all-to-all(bf16[2,128,4,512]{3,2,1,0:T(4,128)(2,1)S(1)} %broadcast_in_dim.19), channel_id=1, replica_groups=mesh['nodes'=128,'rep'=2] {'rep'}, dimensions={0} | all-to-all | bytes 2097152 | tf_op jit(solution)/shard_map/all_to_all | solution.py:16
  58.4 4.2 gather_fusion.1
  65.1 4.2 multiply_convert_fusion.2
  72.6 3.2 copy.34
  75.8 11.1 %scatter_custom_fusion = f32[320,512]{1,0:T(8,128)} fusion(s32[1280]{0:T(1024)S(1)} %copy-done.35, f32[1280,512]{1,0:T(8,128)} %copy.34, f32[]{:T(128)} %constant.13.clone.1), kind=kCustom, calls=%fused_computation.72 | custom fusion | flops 655360 | bytes 655872 | tf_op jit(solution)/shard_map/scatter-add | solution.py:181
  86.9 6.3 %all_to_all.41 = f32[2,160,512]{2,1,0:T(8,128)} all-to-all(f32[2,160,512]{2,1,0:T(8,128)} %bitcast.47), channel_id=1, replica_groups=mesh['nodes'=128,'rep'=2] {'rep'}, dimensions={0} | all-to-all | bytes 1310720 | tf_op jit(solution)/shard_map/all_to_all | solution.py:39
  99.1 4.5 all_to_all.42
  103.6 4.7 %gather_fusion.3 = bf16[1280,512]{1,0:T(8,128)(2,1)} fusion(bf16[320,512]{1,0:T(8,128)(2,1)S(1)} %bitcast.44, s32[2048]{0:T(1024)S(1)} %pad_clamp_fusion), kind=kCustom, calls=%fused_computation.3 | custom fusion | bytes 2626560 | tf_op jit(solution)/shard_map/gather | solution.py:187
  130.2 247.6 %all-reduce.5.cloned.1.call-done = (f32[1536,512]{1,0:T(8,128)}, f32[512,512]{1,0:T(8,128)}, f32[1024,512]{1,0:T(8,128)}, f32[512,512]{1,0:T(8,128)}) async-done(((f32[1536,512]{1,0:T(8,128)}, f32[512,512]{1,0:T(8,128)}, f32[1024,512]{1,0:T(8,128)}, f32[512,512]{1,0:T(8,128)}), (f32[1536,512]{1,0:T(8,128)}, f32[512,512]{1,0:T(8,128)}, f32[1024,512]{1,0:T(8,128)}, ...) | async-done | bytes 7340048 | tf_op jit(solution)/shard_map/psum | solution.py:221
  377.9 3.5 fusion.19
  381.4 10.9 %scatter_custom_fusion.1 = f32[1344,512]{1,0:T(8,128)S(1)} fusion(s32[1280]{0:T(1024)} %param.18, f32[1280,512]{1,0:T(8,128)} %fusion.19, f32[]{:T(128)} %constant.13.clone.1), kind=kCustom, calls=%fused_computation.30 | custom fusion | flops 655360 | bytes 2753024 | tf_op jit(solution)/shard_map/scatter-add | solution.py:201
  398.1 5.5 %all_to_all.43 = bf16[2,128,4,512]{3,2,1,0:T(4,128)(2,1)} all-to-all(bf16[2,128,4,512]{3,2,1,0:T(4,128)(2,1)S(1)} %bitcast.46), channel_id=1, replica_groups=mesh['nodes'=128,'rep'=2] {'rep'}, dimensions={0} | all-to-all | bytes 2097152 | tf_op jit(solution)/shard_map/all_to_all | solution.py:45
  406.5 11.3 %all-to-all-start.6 = ((bf16[128,4,512]{2,1,0:T(4,128)(2,1)}), bf16[128,4,512]{2,1,0:T(4,128)(2,1)}, u32[]{:S(2)}, u32[]{:S(2)}) async-start(bf16[128,4,512]{2,1,0:T(4,128)(2,1)} %reduce_sum.111), calls=%async_computation.6 | async-start | bytes 1048576 | tf_op jit(solution)/shard_map/all_to_all | solution.py:207
  418.0 3.1 fusion.1
  425.1 10.1 %scatter_fusion = f32[320,512]{1,0:T(8,128)S(1)} fusion(f32[320,512]{1,0:T(8,128)S(1)} %slice-done, s32[1280]{0:T(1024)S(1)} %copy-done.35, f32[1280,512]{1,0:T(8,128)S(1)} %fusion.15), kind=kCustom, calls=%fused_computation.6 | custom fusion | flops 655360 | bytes 7869440 | tf_op jit(solution)/shard_map/scatter-add | solution.py:202
  438.6 4.5 scatter_custom_fusion.3
  443.3 4.3 all_to_all.44
  448.6 3.6 multiply_convert_fusion
  (166 shorter events, 63.6 us)
Async XLA Ops:
  7.2 62.2 %copy-start = (bf16[512,512]{1,0:T(8,128)(2,1)S(1)}, bf16[512,512]{1,0:T(8,128)(2,1)}, u32[]{:S(2)}) copy-start(bf16[512,512]{1,0:T(8,128)(2,1)} %param.22) | copy-start | bytes 1572868
  8.9 5.0 %all-to-all-start = ((bf16[2,160,512]{2,1,0:T(8,128)(2,1)}), bf16[2,160,512]{2,1,0:T(8,128)(2,1)S(1)}, u32[]{:S(2)}, u32[]{:S(2)}) async-start(bf16[2,160,512]{2,1,0:T(8,128)(2,1)} %broadcast_in_dim.18), calls=%async_computation | async-start | bytes 655360 | tf_op jit(solution)/shard_map/all_to_all | solution.py:16
  14.0 18.9 %copy-start.35 = (s32[1280]{0:T(1024)S(1)}, s32[1280]{0:T(1024)}, u32[]{:S(2)}) copy-start(s32[1280]{0:T(1024)} %param.19) | copy-start | bytes 15364
  16.8 34.7 %all-to-all-start.1 = ((bf16[128,4,512]{2,1,0:T(4,128)(2,1)}), bf16[128,4,512]{2,1,0:T(4,128)(2,1)}, u32[]{:S(2)}, u32[]{:S(2)}) async-start(bf16[128,4,512]{2,1,0:T(4,128)(2,1)} %reshape.119), calls=%async_computation.1 | async-start | bytes 1048576 | tf_op jit(solution)/shard_map/all_to_all | solution.py:171
  32.7 345.1 %all-reduce.5.cloned.1.call-start = ((), (), s32[]{:S(2)}) async-start(), calls=%async_computation.8 | async-start | bytes 14680064 | tf_op jit(solution)/shard_map/psum | solution.py:221
  32.8 32.3 %collective-permute-start = (bf16[1280,512]{1,0:T(8,128)(2,1)}, bf16[1280,512]{1,0:T(8,128)(2,1)}, u32[]{:S(2)}, u32[]{:S(2)}) collective-permute-start(bf16[1280,512]{1,0:T(8,128)(2,1)} %param.15), channel_id=1, source_target_pairs={{0,1},{1,0},{2,3},{3,2},{4,5},{5,4},{6,7},{7,6},{8,9},{9,8},{10,11... | collective-permute-start | bytes 3932168 | tf_op jit(solution)/shard_map/ppermute | solution.py:11
  37.0 7.9 %copy-start.5 = (bf16[1280,512]{1,0:T(8,128)(2,1)}, bf16[1280,512]{1,0:T(8,128)(2,1)S(1)}, u32[]{:S(2)}) copy-start(bf16[1280,512]{1,0:T(8,128)(2,1)S(1)} %gather_fusion.2) | copy-start | bytes 3932164
  62.7 6.7 %copy-start.7 = (bf16[1280,512]{1,0:T(8,128)(2,1)}, bf16[1280,512]{1,0:T(8,128)(2,1)S(1)}, u32[]{:S(2)}) copy-start(bf16[1280,512]{1,0:T(8,128)(2,1)S(1)} %gather_fusion.1) | copy-start | bytes 3932164
  86.9 10.8 %copy-start.27 = (bf16[160,512]{1,0:T(8,128)(2,1)S(1)}, bf16[160,512]{1,0:T(8,128)(2,1)}, u32[]{:S(2)}) copy-start(bf16[160,512]{1,0:T(8,128)(2,1)} %param.16) | copy-start | bytes 491524
  86.9 10.8 %copy-start.39 = (f32[512]{0:T(512)S(1)}, f32[512]{0:T(512)}, u32[]{:S(2)}) copy-start(f32[512]{0:T(512)} %param.27) | copy-start | bytes 6148
  94.4 4.0 copy-start.17
  94.4 3.6 copy-start.28
  97.5 6.1 %copy-start.21 = (f32[160,512]{1,0:T(8,128)}, f32[160,512]{1,0:T(8,128)S(1)}, u32[]{:S(2)}) copy-start(f32[160,512]{1,0:T(8,128)S(1)} %get-tuple-element.41) | copy-start | bytes 983044
  97.9 10.3 %copy-start.40 = (f32[160]{0:T(256)}, f32[160]{0:T(256)S(1)}, u32[]{:S(2)}) copy-start(f32[160]{0:T(256)S(1)} %get-tuple-element.42) | copy-start | bytes 1924
  98.0 10.3 %copy-start.42 = (f32[160]{0:T(256)}, f32[160]{0:T(256)S(1)}, u32[]{:S(2)}) copy-start(f32[160]{0:T(256)S(1)} %get-tuple-element.43) | copy-start | bytes 1924
  116.7 261.2 %copy-start.9 = (bf16[1280,512]{1,0:T(8,128)(2,1)}, bf16[1280,512]{1,0:T(8,128)(2,1)S(1)}, u32[]{:S(2)}) copy-start(bf16[1280,512]{1,0:T(8,128)(2,1)S(1)} %fusion.2) | copy-start | bytes 3932164
  130.0 318.6 %all-reduce.7.cloned.1.call-start = ((), (), s32[]{:S(2)}) async-start(), calls=%async_computation.9 | async-start | bytes 14680064 | tf_op jit(solution)/shard_map/psum | solution.py:221
  392.3 25.7 %copy-start.2 = (f32[1344,512]{1,0:T(8,128)}, f32[1344,512]{1,0:T(8,128)S(1)}, u32[]{:S(2)}) copy-start(f32[1344,512]{1,0:T(8,128)S(1)} %scatter_custom_fusion.1) | copy-start | bytes 8257540
  398.1 19.7 %copy-start.32 = (s32[1,128,4]{2,1,0:T(8,128)S(1)}, s32[1,128,4]{2,1,0:T(8,128)}, u32[]{:S(2)}) copy-start(s32[1,128,4]{2,1,0:T(8,128)} %copy-done.31) | copy-start | bytes 6148
  406.5 30.0 %all-to-all-start.6 = ((bf16[128,4,512]{2,1,0:T(4,128)(2,1)}), bf16[128,4,512]{2,1,0:T(4,128)(2,1)}, u32[]{:S(2)}, u32[]{:S(2)}) async-start(bf16[128,4,512]{2,1,0:T(4,128)(2,1)} %reduce_sum.111), calls=%async_computation.6 | async-start | bytes 1048576 | tf_op jit(solution)/shard_map/all_to_all | solution.py:207
  438.6 8.9 %copy-start.13 = (bf16[1024,512]{1,0:T(8,128)(2,1)S(1)}, bf16[1024,512]{1,0:T(8,128)(2,1)}, u32[]{:S(2)}) copy-start(bf16[1024,512]{1,0:T(8,128)(2,1)} %param.25) | copy-start | bytes 3145732
  438.6 8.9 %copy-start.30 = (bf16[160,512]{1,0:T(8,128)(2,1)S(1)}, bf16[160,512]{1,0:T(8,128)(2,1)}, u32[]{:S(2)}) copy-start(bf16[160,512]{1,0:T(8,128)(2,1)} %param.16) | copy-start | bytes 491524
  448.6 3.6 copy-start.26
  448.6 4.6 copy-start.14
  (29 other events, 57.1 us)
Sparse Core Ops, SparseCore 0:
  130.1 247.6 all-reduce.4
  381.2 43.4 all-reduce.6
